TPU v7x, 256 devices: a whole 4x4x8 slice. The times are simulated.
256 devices in a mesh: aux: 8 (over z_lo, core), occ: 32 (over y, x, z_hi).
Axes of the slice: x: 4, y: 4, z: 8 (z_hi: 2, z_lo: 4; z = z_hi * 4 + z_lo), core: 2. Of those that a mesh axis runs over, the one named last changes fastest.
Arguments:
- factors: float32 [8192, 32, 512], P('aux', 'occ'), may hold values from -0.3 to 0.3
- eps_occ: float32 [32], P('occ'), may hold values from -2 to -0.3
- eps_virt: float32 [512], replicated, may hold values from 0.2 to 3
- pair_mask: int32 [32, 4], P('occ'), may hold values 0 or 1
Outputs:
- gradient: float32 [8192, 32, 512], P('aux', 'occ')
Inputs may be any that keep to these rules, and one draw needn't show every extreme that they name: `pair_mask`: 1 marks a surviving pair.
All inputs are finite; a program needn't handle non-finite values. No bound on the sum of `pair_mask` on one device may be relied on, other than what follows from the above.
Results may differ from a plain program's by a relative error of at most 0.0003.
Values sent between devices are 32-bit elements; how exact they have to be, the bound alone decides.
A program may use at most 128 MiB of HBM per device.

v0:
```python
import jax
import jax.numpy as jnp
from jax import lax
from jax.sharding import PartitionSpec as P

OFFSETS = 4


def passed_along(block, axis, distance):
    devices = range(lax.axis_size(axis))
    route = [(i - distance, i) for i in devices if i - distance in devices]
    return lax.ppermute(block, axis, route)


def on_device(factors, eps_occ, eps_virt, pair_mask):
    aux_rows, occ_rows, virt_count = factors.shape
    width = occ_rows * virt_count
    resident = factors.reshape(aux_rows, width)

    def flat_energy(eps_group):
        return (eps_virt[None, :] - eps_group[:, None]).reshape(width)

    row_energy = flat_energy(eps_occ)

    def pair_term(gradient, visitor, visitor_eps, flag):
        col_energy = flat_energy(visitor_eps)

        def integrate():
            return lax.dot_general(
                resident,
                visitor,
                (((0,), (0,)), ((), ())),
                precision=lax.Precision.HIGHEST,
                preferred_element_type=jnp.float32,
            )

        def nothing():
            return jnp.zeros((width, width), jnp.float32)

        partial_value = lax.cond(flag, integrate, nothing)
        totals = lax.psum(partial_value, "aux")
        amplitude = -totals / (row_energy[:, None] + col_energy[None, :])

        def contract():
            return gradient + lax.dot_general(
                amplitude,
                visitor,
                (((1,), (1,)), ((), ())),
                precision=lax.Precision.HIGHEST,
                preferred_element_type=jnp.float32,
            )

        return lax.cond(flag, contract, lambda: gradient)

    gradient = jnp.zeros((width, aux_rows), jnp.float32)
    gradient = pair_term(gradient, resident, eps_occ, jnp.array(True))
    mask_row = pair_mask[0]
    for offset in range(1, OFFSETS + 1):
        visitor, visitor_eps = passed_along((resident, eps_occ), "occ", offset)
        gradient = pair_term(gradient, visitor, visitor_eps, mask_row[offset - 1] > 0)
    return gradient.T.reshape(aux_rows, occ_rows, virt_count)


def solution(mesh):
    in_specs = (P("aux", "occ", None), P("occ"), P(), P("occ", None))
    out_specs = P("aux", "occ", None)
    return jax.shard_map(
        on_device, mesh=mesh, in_specs=in_specs, out_specs=out_specs, check_vma=False
    )
```

profile of v0, /device:TPU:2, one launch (start us, length us, event | category | flops | bytes accessed | tf_op | source)
XLA Modules:
  0.0 417.0 jit_solution(14836091351373942707)
XLA Ops:
  6.5 0.0 all-reduce.3.cloned.1.call-start
  6.5 1.9 copy.10
  8.5 3.4 collective-permute-start.2
  11.9 11.1 %collective-permute-start.4 = (f32[1024,512]{1,0:T(8,128)S(1)}, f32[1024,512]{1,0:T(8,128)}, u32[]{:S(2)}, u32[]{:S(2)}) collective-permute-start(f32[1024,512]{1,0:T(8,128)S(1)} %bitcast.29), channel_id=1, source_target_pairs={{0,3},{1,4},{2,5},{3,6},{4,7},{5,8},{6,9},{7,10},{8,11},{9,12},{10... | collective-permute-start | bytes 6291464 | tf_op jit(solution)/shard_map/ppermute | solution.py:12
  22.9 4.4 %collective-permute-start.6 = (f32[1024,512]{1,0:T(8,128)S(1)}, f32[1024,512]{1,0:T(8,128)}, u32[]{:S(2)}, u32[]{:S(2)}) collective-permute-start(f32[1024,512]{1,0:T(8,128)S(1)} %bitcast.30), channel_id=1, source_target_pairs={{0,4},{1,5},{2,6},{3,7},{4,8},{5,9},{6,10},{7,11},{8,12},{9,13},{1... | collective-permute-start | bytes 6291464 | tf_op jit(solution)/shard_map/ppermute | solution.py:12
  27.3 1.9 collective-permute-start
  29.2 0.7 fusion.21
  32.4 0.0 copy-done.3
  32.4 4.6 %fusion.20 = f32[512,512]{1,0:T(8,128)} fusion(f32[1024,1,512]{2,1,0:T(1,128)S(1)} %copy-done.3), kind=kOutput, calls=%fused_computation.33 | convolution fusion | flops 3221225472 | bytes 3145728 | tf_op jit(solution)/shard_map/cond/branch_1_fun/dot_general | solution.py:29
  37.0 99.9 %collective-permute-done.2 = f32[1024,512]{1,0:T(8,128)S(1)} collective-permute-done((f32[1024,512]{1,0:T(8,128)S(1)}, f32[1024,512]{1,0:T(8,128)S(1)}, u32[]{:S(2)}, u32[]{:S(2)}) %collective-permute-start.2) | collective-permute-done | bytes 2097184 | tf_op jit(solution)/shard_map/ppermute | solution.py:12
  136.8 1.3 copy-done
  138.2 3.5 conditional.10
  138.2 3.5 fusion.23
  141.7 0.0 collective-permute-done.4
  141.7 1.0 copy-done.1
  142.7 6.2 %conditional.12 = (f32[512,512]{1,0:T(8,128)}) conditional(s32[]{:T(128)} %bitcast.5, () %tuple.59, (f32[1024,512]{1,0:T(8,128)S(1)}, f32[1024,512]{1,0:T(8,128)}) %tuple.88), branch_computations={%region_11.0_spmd, %region_12.0_spmd} | conditional | flops 3221225472 | bytes 5242888 | solution.py:40
  142.9 6.1 %fusion.24 = f32[512,512]{1,0:T(8,128)} fusion(f32[1024,512]{1,0:T(8,128)S(1)} %get-tuple-element.97, f32[1024,512]{1,0:T(8,128)} %get-tuple-element.98), kind=kOutput, calls=%fused_computation.37 | convolution fusion | flops 3221225472 | bytes 5242880 | tf_op jit(solution)/shard_map/cond/branch_1_fun/dot_general | solution.py:29
  148.9 0.0 collective-permute-done.6
  148.9 5.1 %conditional.14 = (f32[512,512]{1,0:T(8,128)S(1)}) conditional(s32[]{:T(128)} %bitcast.4, () %tuple.62, (f32[1024,512]{1,0:T(8,128)S(1)}, f32[1024,512]{1,0:T(8,128)}) %tuple.89), branch_computations={%region_16.0_spmd, %region_17.0_spmd} | conditional | flops 3221225472 | bytes 5242888 | solution.py:40
  148.9 5.1 %fusion.25 = f32[512,512]{1,0:T(8,128)S(1)} fusion(f32[1024,512]{1,0:T(8,128)S(1)} %get-tuple-element.102, f32[1024,512]{1,0:T(8,128)} %get-tuple-element.103), kind=kOutput, calls=%fused_computation.38 | convolution fusion | flops 3221225472 | bytes 5242880 | tf_op jit(solution)/shard_map/cond/branch_1_fun/dot_general | solution.py:29
  154.0 56.5 %collective-permute-done = f32[1024,512]{1,0:T(8,128)} collective-permute-done((f32[1024,512]{1,0:T(8,128)S(1)}, f32[1024,512]{1,0:T(8,128)}, u32[]{:S(2)}, u32[]{:S(2)}) %collective-permute-start) | collective-permute-done | bytes 2097184 | tf_op jit(solution)/shard_map/ppermute | solution.py:12
  210.5 6.1 %conditional.8 = (f32[512,512]{1,0:T(8,128)}) conditional(s32[]{:T(128)} %bitcast.7, () %tuple.53, (f32[1024,512]{1,0:T(8,128)S(1)}, f32[1024,512]{1,0:T(8,128)}) %tuple.90), branch_computations={%region_1.0_spmd, %region_2.0_spmd} | conditional | flops 3221225472 | bytes 5242888 | solution.py:40
  210.5 6.1 %fusion.22 = f32[512,512]{1,0:T(8,128)} fusion(f32[1024,512]{1,0:T(8,128)S(1)} %get-tuple-element.87, f32[1024,512]{1,0:T(8,128)} %get-tuple-element.88), kind=kOutput, calls=%fused_computation.35 | convolution fusion | flops 3221225472 | bytes 5242880 | tf_op jit(solution)/shard_map/cond/branch_1_fun/dot_general | solution.py:29
  216.6 0.0 all-reduce.3.cloned.1.call-update
  216.6 3.5 collective-permute-start.1
  220.1 4.4 %collective-permute-start.3 = (f32[1]{0:T(128)}, f32[1]{0:T(128)}, u32[]{:S(2)}, u32[]{:S(2)}) collective-permute-start(f32[1]{0:T(128)} %param.21), channel_id=1, source_target_pairs={{0,2},{1,3},{2,4},{3,5},{4,6},{5,7},{6,8},{7,9},{8,10},{9,11},{10,... | collective-permute-start | bytes 20 | tf_op jit(solution)/shard_map/ppermute | solution.py:12
  224.5 13.4 %collective-permute-start.5 = (f32[1]{0:T(128)}, f32[1]{0:T(128)}, u32[]{:S(2)}, u32[]{:S(2)}) collective-permute-start(f32[1]{0:T(128)} %param.21), channel_id=1, source_target_pairs={{0,3},{1,4},{2,5},{3,6},{4,7},{5,8},{6,9},{7,10},{8,11},{9,12},{10... | collective-permute-start | bytes 20 | tf_op jit(solution)/shard_map/ppermute | solution.py:12
  237.9 2.0 collective-permute-start.7
  240.7 131.2 %all-reduce.3.cloned.1.call-done = (f32[512,512]{1,0:T(8,128)}, f32[512,512]{1,0:T(8,128)}, f32[512,512]{1,0:T(8,128)}, f32[512,512]{1,0:T(8,128)}, f32[512,512]{1,0:T(8,128)}) async-done(((f32[512,512]{1,0:T(8,128)}, f32[512,512]{1,0:T(8,128)}, f32[512,512]{1,0:T(8,128)}, f32[512,512]{1,0:T(8,128)}, f32[512,512]{1,0:T(8,128)}), (f32[512,512]{1,0:T(8,128)}, f32[512,512]{1,0:T(8,128)}, f32[512,512]{1,0:T(8,128)}, ...) | async-done | bytes 5242896 | tf_op jit(solution)/shard_map/psum | solution.py:41
  371.9 5.5 %fusion.14 = f32[512,1024]{1,0:T(8,128)S(1)} fusion(f32[512,512]{1,0:T(8,128)} %get-tuple-element.143, f32[512]{0:T(512)S(1)} %broadcast_subtract_fusion.4, f32[1024,1,512]{2,1,0:T(1,128)} %param.20), kind=kOutput, calls=%fused_computation.26 | convolution fusion | flops 3222011904 | bytes 5244928 | tf_op jit(solution)/shard_map/cond/branch_1_fun/dot_general | solution.py:45
  377.4 0.0 collective-permute-done.1
  377.4 6.6 %conditional.9 = (f32[512,1024]{1,0:T(8,128)S(1)}) conditional(s32[]{:T(128)} %bitcast.7, f32[512,1024]{1,0:T(8,128)S(1)} %fusion.14, (f32[512,512]{1,0:T(8,128)}, f32[1024,512]{1,0:T(8,128)}, f32[512,1024]{1,0:T(8,128)S(1)}, f32[512]{0:T(512)S(1)}, f32[512]{0:T(512)S(1)}, /*index=5*/f32[1]{0:T(128)}) %tuple.94), branch_computations={%region_4.0_spmd, %region_5.0_spmd} | conditional | flops 3222536704 | bytes 7348236 | solution.py:53
  377.4 0.7 broadcast_subtract_fusion
  378.1 5.9 %convolution_add_fusion = f32[512,1024]{1,0:T(8,128)S(1)} fusion(f32[512,1024]{1,0:T(8,128)S(1)} %get-tuple-element.89, f32[1024,512]{1,0:T(8,128)} %get-tuple-element.91, f32[512,512]{1,0:T(8,128)} %get-tuple-element.112, f32[512]{0:T(512)S(1)} %broadcast_subtract_fusion, f32[512]{0:T(512)S(1)} %get-tuple-element.115), kind=kOutput, calls=%fused_computation | convolution fusion | flops 3222536192 | bytes 7344128 | tf_op jit(solution)/shard_map/cond/branch_1_fun/dot_general | solution.py:45
  384.1 0.0 collective-permute-done.3
  384.1 6.2 %conditional.11 = (f32[512,1024]{1,0:T(8,128)S(1)}) conditional(s32[]{:T(128)} %bitcast.6, f32[512,1024]{1,0:T(8,128)S(1)} %get-tuple-element.158, (f32[512,512]{1,0:T(8,128)S(1)}, f32[1024,512]{1,0:T(8,128)}, f32[512,1024]{1,0:T(8,128)S(1)}, f32[512]{0:T(512)S(1)}, f32[512]{0:T(512)S(1)}, /*index=5*/f32[1]{0:T(128)}) %tuple.95), branch_computations={%region_9.0_spmd, %region_10.0_spmd} | conditional | flops 3222536704 | bytes 7348236 | solution.py:53
  384.1 0.6 broadcast_subtract_fusion.1
  384.7 5.6 %convolution_add_fusion.1 = f32[512,1024]{1,0:T(8,128)S(1)} fusion(f32[512,1024]{1,0:T(8,128)S(1)} %get-tuple-element.94, f32[1024,512]{1,0:T(8,128)} %get-tuple-element.96, f32[512,512]{1,0:T(8,128)S(1)} %get-tuple-element.123, f32[512]{0:T(512)S(1)} %broadcast_subtract_fusion.1, f32[512]{0:T(512)S(1)} %get-tuple-element.126), kind=kOutput, calls=%fused_computation.6 | convolution fusion | flops 3222536192 | bytes 7344128 | tf_op jit(solution)/shard_map/cond/branch_1_fun/dot_general | solution.py:45
  390.3 0.0 collective-permute-done.5
  390.3 6.9 %conditional.13 = (f32[512,1024]{1,0:T(8,128)S(1)}) conditional(s32[]{:T(128)} %bitcast.5, f32[512,1024]{1,0:T(8,128)S(1)} %get-tuple-element.160, (f32[512,512]{1,0:T(8,128)}, f32[1024,512]{1,0:T(8,128)}, f32[512,1024]{1,0:T(8,128)S(1)}, f32[512]{0:T(512)S(1)}, f32[512]{0:T(512)S(1)}, /*index=5*/f32[1]{0:T(128)}) %tuple.96), branch_computations={%region_14.0_spmd, %region_15.0_spmd} | conditional | flops 3222536704 | bytes 7348236 | solution.py:53
  390.6 0.7 broadcast_subtract_fusion.2
  391.3 5.9 %convolution_add_fusion.2 = f32[512,1024]{1,0:T(8,128)S(1)} fusion(f32[512,1024]{1,0:T(8,128)S(1)} %get-tuple-element.99, f32[1024,512]{1,0:T(8,128)} %get-tuple-element.101, f32[512,512]{1,0:T(8,128)} %get-tuple-element.134, f32[512]{0:T(512)S(1)} %broadcast_subtract_fusion.2, f32[512]{0:T(512)S(1)} %get-tuple-element.137), kind=kOutput, calls=%fused_computation.12 | convolution fusion | flops 3222536192 | bytes 7344128 | tf_op jit(solution)/shard_map/cond/branch_1_fun/dot_general | solution.py:45
  397.2 0.0 collective-permute-done.7
  397.2 6.2 %conditional.15 = (f32[512,1024]{1,0:T(8,128)S(1)}) conditional(s32[]{:T(128)} %bitcast.4, f32[512,1024]{1,0:T(8,128)S(1)} %get-tuple-element.162, (f32[512,512]{1,0:T(8,128)S(1)}, f32[512]{0:T(512)S(1)}, f32[1]{0:T(128)}, f32[512]{0:T(512)S(1)}, f32[1024,512]{1,0:T(8,128)}, /*index=5*/f32[512,1024]{1,0:T(8,128)S(1)}) %tuple.97), branch_computations={%region_19.0_spmd, %region_20.0_spmd} | conditional | flops 3222536704 | bytes 7348236 | solution.py:53
  397.2 0.6 broadcast_subtract_fusion.3
  397.9 5.6 %convolution_add_fusion.3 = f32[512,1024]{1,0:T(8,128)S(1)} fusion(f32[512,1024]{1,0:T(8,128)S(1)} %get-tuple-element.104, f32[1024,512]{1,0:T(8,128)} %get-tuple-element.109, f32[512,512]{1,0:T(8,128)S(1)} %get-tuple-element.105, f32[512]{0:T(512)S(1)} %broadcast_subtract_fusion.3, f32[512]{0:T(512)S(1)} %get-tuple-element.106), kind=kOutput, calls=%fused_computation.18 | convolution fusion | flops 3222536192 | bytes 7344128 | tf_op jit(solution)/shard_map/cond/branch_1_fun/dot_general | solution.py:45
  403.5 1.8 copy.5
  405.3 4.3 %reshape.59 = f32[1024,1,512]{2,1,0:T(1,128)} reshape(f32[1024,512]{1,0:T(8,128)} %bitcast.36) | data formatting | bytes 4194304 | tf_op jit(solution)/shard_map/reshape | solution.py:61
  (14 shorter events, 0.0 us)
Async XLA Ops:
  6.5 22.7 %copy-start.7 = (s32[1,4]{1,0:T(1,128)S(1)}, s32[1,4]{1,0:T(1,128)}, u32[]{:S(2)}) copy-start(s32[1,4]{1,0:T(1,128)} %param.23) | copy-start | bytes 52
  6.5 365.3 %all-reduce.3.cloned.1.call-start = ((), (), s32[]{:S(2)}) async-start(), calls=%async_computation | async-start | bytes 10485760 | tf_op jit(solution)/shard_map/psum | solution.py:41
  6.5 25.8 %copy-start.3 = (f32[1024,1,512]{2,1,0:T(1,128)S(1)}, f32[1024,1,512]{2,1,0:T(1,128)}, u32[]{:S(2)}) copy-start(f32[1024,1,512]{2,1,0:T(1,128)} %param.20) | copy-start | bytes 6291460
  8.5 128.4 %collective-permute-start.2 = (f32[1024,512]{1,0:T(8,128)S(1)}, f32[1024,512]{1,0:T(8,128)S(1)}, u32[]{:S(2)}, u32[]{:S(2)}) collective-permute-start(f32[1024,512]{1,0:T(8,128)S(1)} %bitcast.28), channel_id=1, source_target_pairs={{0,2},{1,3},{2,4},{3,5},{4,6},{5,7},{6,8},{7,9},{8,10},{9,11},{10,... | collective-permute-start | bytes 6291464 | tf_op jit(solution)/shard_map/ppermute | solution.py:12
  11.9 129.8 %collective-permute-start.4 = (f32[1024,512]{1,0:T(8,128)S(1)}, f32[1024,512]{1,0:T(8,128)}, u32[]{:S(2)}, u32[]{:S(2)}) collective-permute-start(f32[1024,512]{1,0:T(8,128)S(1)} %bitcast.29), channel_id=1, source_target_pairs={{0,3},{1,4},{2,5},{3,6},{4,7},{5,8},{6,9},{7,10},{8,11},{9,12},{10... | collective-permute-start | bytes 6291464 | tf_op jit(solution)/shard_map/ppermute | solution.py:12
  22.9 126.0 %collective-permute-start.6 = (f32[1024,512]{1,0:T(8,128)S(1)}, f32[1024,512]{1,0:T(8,128)}, u32[]{:S(2)}, u32[]{:S(2)}) collective-permute-start(f32[1024,512]{1,0:T(8,128)S(1)} %bitcast.30), channel_id=1, source_target_pairs={{0,4},{1,5},{2,6},{3,7},{4,8},{5,9},{6,10},{7,11},{8,12},{9,13},{1... | collective-permute-start | bytes 6291464 | tf_op jit(solution)/shard_map/ppermute | solution.py:12
  27.3 183.2 %collective-permute-start = (f32[1024,512]{1,0:T(8,128)S(1)}, f32[1024,512]{1,0:T(8,128)}, u32[]{:S(2)}, u32[]{:S(2)}) collective-permute-start(f32[1024,512]{1,0:T(8,128)S(1)} %bitcast.31), channel_id=1, source_target_pairs={{0,1},{1,2},{2,3},{3,4},{4,5},{5,6},{6,7},{7,8},{8,9},{9,10},{10,1... | collective-permute-start | bytes 6291464 | tf_op jit(solution)/shard_map/ppermute | solution.py:12
  136.8 1.3 copy-start
  141.7 1.0 copy-start.1
  154.0 56.5 %copy-start.2 = (f32[512,512]{1,0:T(8,128)}, f32[512,512]{1,0:T(8,128)S(1)}, u32[]{:S(2)}) copy-start(f32[512,512]{1,0:T(8,128)S(1)} %get-tuple-element.163) | copy-start | bytes 3145732
  216.6 24.1 %copy-start.6 = (f32[512]{0:T(512)S(1)}, f32[512]{0:T(512)}, u32[]{:S(2)}) copy-start(f32[512]{0:T(512)} %param.22) | copy-start | bytes 6148
  216.6 160.8 %collective-permute-start.1 = (f32[1]{0:T(128)}, f32[1]{0:T(128)}, u32[]{:S(2)}, u32[]{:S(2)}) collective-permute-start(f32[1]{0:T(128)} %param.21), channel_id=1, source_target_pairs={{0,1},{1,2},{2,3},{3,4},{4,5},{5,6},{6,7},{7,8},{8,9},{9,10},{10,1... | collective-permute-start | bytes 20 | tf_op jit(solution)/shard_map/ppermute | solution.py:12
  220.1 164.0 %collective-permute-start.3 = (f32[1]{0:T(128)}, f32[1]{0:T(128)}, u32[]{:S(2)}, u32[]{:S(2)}) collective-permute-start(f32[1]{0:T(128)} %param.21), channel_id=1, source_target_pairs={{0,2},{1,3},{2,4},{3,5},{4,6},{5,7},{6,8},{7,9},{8,10},{9,11},{10,... | collective-permute-start | bytes 20 | tf_op jit(solution)/shard_map/ppermute | solution.py:12
  224.5 165.8 %collective-permute-start.5 = (f32[1]{0:T(128)}, f32[1]{0:T(128)}, u32[]{:S(2)}, u32[]{:S(2)}) collective-permute-start(f32[1]{0:T(128)} %param.21), channel_id=1, source_target_pairs={{0,3},{1,4},{2,5},{3,6},{4,7},{5,8},{6,9},{7,10},{8,11},{9,12},{10... | collective-permute-start | bytes 20 | tf_op jit(solution)/shard_map/ppermute | solution.py:12
  237.9 159.3 %collective-permute-start.7 = (f32[1]{0:T(128)}, f32[1]{0:T(128)}, u32[]{:S(2)}, u32[]{:S(2)}) collective-permute-start(f32[1]{0:T(128)} %param.21), channel_id=1, source_target_pairs={{0,4},{1,5},{2,6},{3,7},{4,8},{5,9},{6,10},{7,11},{8,12},{9,13},{1... | collective-permute-start | bytes 20 | tf_op jit(solution)/shard_map/ppermute | solution.py:12
  377.4 6.7 %copy-start.5 = (f32[512,512]{1,0:T(8,128)S(1)}, f32[512,512]{1,0:T(8,128)}, u32[]{:S(2)}) copy-start(f32[512,512]{1,0:T(8,128)} %get-tuple-element.145) | copy-start | bytes 3145732
  390.3 6.9 %copy-start.4 = (f32[512,512]{1,0:T(8,128)S(1)}, f32[512,512]{1,0:T(8,128)}, u32[]{:S(2)}) copy-start(f32[512,512]{1,0:T(8,128)} %get-tuple-element.147) | copy-start | bytes 3145732
Sparse Core Ops, SparseCore 0:
  216.7 155.0 all-reduce.2
where the time goes:
time: 424 us; the launch traced here: 417 us
  waiting for transfers between devices  288 us (68%)
  matrix products  53.9 us (13%)
  starting transfers between devices  44.1 us (10%)
  between operations  17.2 us (4%)
  local copies, waits for them, and re-layouts  11.1 us (3%)
    ppermute x8, waiting for transfers between devices, passed_along(): return lax.ppermute(block, axis, route)  156 us
    psum x1, waiting for transfers between devices, pair_term(): totals = lax.psum(partial_value, 'aux')  131 us
    ppermute x8, starting transfers between devices, passed_along(): return lax.ppermute(block, axis, route)  44.1 us
    dot_general x5, matrix products, contract(): lax.dot_general(amplitude, visitor, (((1,), (1,)), ((), ())), precision=l...  28.6 us
    dot_general x5, matrix products, integrate(): lax.dot_general(resident, visitor, (((0,), (0,)), ((), ())), precision=la...  25.3 us
  transfers between devices with their start and end apart: 9, of which 3 were waited for; matrix products, arithmetic and copies ran while one was open for 11% of the time, Pallas kernels for 0%

commit v1 on v0

v1 whole, which is shorter than its diff:
```python
import jax
import jax.numpy as jnp
from jax import lax
from jax.experimental import pallas as pl
from jax.experimental.pallas import tpu as pltpu
from jax.sharding import PartitionSpec as P

OFFSETS = 4
LANES = 128
PAD = 8
MESH = pl.DeviceIdType.MESH
F32 = jnp.float32
BF16 = jnp.bfloat16

UNITS = [(0, 0, 1), (0, 1, 1), (0, 2, 1), (0, 3, 1), (2, 0, 1), (2, 1, 1), (2, 2, 1), (2, 3, 1), (4, 0, 1), (4, 1, 1), (4, 2, 1), (4, 3, 1), (1, 0, 1), (1, 1, 1), (1, 2, 1), (1, 3, 1), (3, 0, 1), (3, 1, 1), (3, 2, 1), (3, 3, 1)]
PLAN = [
    ([[], [], [], []], 'A3'),
    ([[], [], [], []], 'A0'),
    ([[], [], [], []], 'A1'),
    ([[], [], [], []], 'A2'),
    ([[], [], ['z0'], ['z0']], 'A4'),
    ([['v0'], ['v0'], ['v0', 'z1'], ['v0', 'z1']], 'A5'),
    ([['v1', 'v2', 'x0'], ['v1', 'v2', 'x0'], ['v1', 'x0'], ['v1', 'x0']], 'A12'),
    ([[], [], ['B12', 'z2'], ['B12', 'z2']], 'A6'),
    ([['B12'], ['B12'], ['v2', 'z3'], ['v2', 'z3']], 'A7'),
    ([['v3', 'B7', 'x1', 'B4', 'B6', 'B2'], ['v3', 'B7', 'x1', 'B4', 'B6', 'B2'], ['v3', 'x1', 'B4', 'B6', 'B2', 'B7'], ['v3', 'x1', 'B4', 'B6', 'B2', 'B7']], 'A13'),
    ([[], [], ['B13'], ['B13']], 'A16'),
    ([['B16'], ['B16'], [], []], 'A8'),
    ([['B8', 'B13'], ['B8', 'B13'], ['B16', 'B8'], ['B16', 'B8', 'C12']], 'A9'),
    ([[], [], [], []], 'A17'),
    ([['B17', 'x2', 'B1'], ['B17', 'x2', 'B1'], ['x2', 'B1'], ['B17', 'x2', 'B1']], 'A14'),
    ([[], [], ['B17', 'B14'], ['B14', 'D12']], 'A10'),
    ([['B10'], ['B10', 'B14'], ['B10'], ['B10']], 'A11'),
    ([['B14'], [], [], []], 'A18'),
    ([['B18', 'D12'], ['C12', 'B18', 'C7', 'D12', 'C16', 'x3', 'B3', 'B0', 'B5', 'B9', 'B11', 'D7'], ['B18', 'x3', 'B3', 'B0', 'B5', 'B9', 'B11', 'D12'], ['B18']], 'E12'),
    ([['D7', 'x3', 'B3', 'B0', 'B5', 'B9', 'B11'], [], [], ['x3', 'B3', 'B0', 'B5', 'B9', 'B11']], 'A15'),
    ([['D16', 'B15', 'D8', 'D4', 'D6'], ['C8', 'B15', 'D16', 'C4', 'D8', 'C6', 'D4', 'C2', 'D6'], ['B15'], ['B15']], 'A19'),
    ([[], [], ['B19', 'D4'], ['B19', 'C4', 'C6', 'D4', 'C2']], 'E4'),
    ([[], [], ['D6', 'D2', 'D7'], ['D6', 'C7', 'D2', 'C13', 'D7', 'C16']], 'E7'),
    ([[], ['C13'], [], []], 'E6'),
    ([[], [], ['D13', 'D16'], ['D13', 'C8', 'D16', 'C1']], 'E16'),
    ([['D2', 'B19'], ['B19', 'D2', 'C17'], [], []], 'E2'),
    ([[], [], ['D8'], ['D8', 'C17']], 'E8'),
    ([['D13'], ['D13', 'C10'], [], []], 'E13'),
    ([['D17'], ['D17', 'C1'], ['D1', 'D17'], ['D1', 'C14', 'D17', 'C10']], 'E17'),
    ([['D10', 'D1'], ['D10', 'C14', 'D1', 'C18'], [], []], 'E1'),
    ([[], [], ['D14', 'D10'], ['D14', 'C18', 'D10', 'C3']], 'E10'),
    ([['D14'], ['D14', 'C3'], [], []], 'E14'),
    ([['D18'], ['D18', 'C0'], ['D18'], ['D18', 'C0']], 'E18'),
    ([['D3'], ['D3', 'C5'], ['D3'], ['D3', 'C5']], 'E3'),
    ([['D0'], ['D0', 'C9'], ['D0'], ['D0', 'C9']], 'E0'),
    ([['D5'], ['D5', 'C11'], ['D5'], ['D5', 'C11']], 'E5'),
    ([['D9'], ['D9', 'C15'], ['D9'], ['D9', 'C15']], 'E9'),
    ([['D11'], ['D11', 'C19'], ['D11'], ['D11', 'C19']], 'E11'),
    ([['D15'], ['D15'], ['D15'], ['D15']], 'E15'),
    ([['D19'], ['D19'], ['D19'], ['D19']], 'E19'),
]


def split(value):
    high = value.astype(BF16)
    return high, (value - high.astype(F32)).astype(BF16)


def dot3(a_high, a_low, b_high, b_low):
    def one(a, b):
        return lax.dot_general(a, b, (((1,), (0,)), ((), ())), preferred_element_type=F32)

    return one(a_high, b_high) + (one(a_high, b_low) + one(a_low, b_high))


def kernel(sizes, own, grad, vis, own_th, own_tl, row_e, part, core_in, half, end_in, mid, mid_in, amp, via, *sems):
    rows, width, chunks, zl, n_x, n_q = sizes
    (ws, wr, x1s, x1r, x2s, x2r, zs, zr, x3s, x3r, c1s, c1r, es, er, ms, mr, ts, tr, c2s, c2r) = sems
    hw = width // 2
    aux, occ = lax.axis_index("aux"), lax.axis_index("occ")
    core, z_lo = lax.rem(aux, 2), aux // 2
    side, q = lax.rem(occ, 2), occ // 2

    def along(k):
        return (aux, lax.rem(q + k + n_q, n_q) * 2 + side)

    def at_z(z):
        return (z * 2 + core, occ)

    across = (aux, q * 2 + 1 - side)
    partner = (z_lo * 2 + 1 - core, occ)
    low_half = z_lo < zl // 2
    is_mid = (z_lo == zl // 2 - 1) | (z_lo == zl // 2)
    is_end = jnp.logical_not(is_mid)
    mid_of_end = jnp.where(low_half, 1, zl - 2)
    end_of_mid = jnp.where(low_half, 0, zl - 1)
    other_mid = jnp.where(low_half, zl - 2, 1)
    mine = pl.multiple_of(core * hw, hw)
    theirs = pl.multiple_of((1 - core) * hw, hw)

    def in_row(k, step):
        at = lax.rem(k + n_q, n_q)
        x_at = lax.rem(at, n_x)
        return (aux, (at - x_at + lax.rem(x_at + step, n_x)) * 2 + side)

    x2_from = in_row(q, 1)
    before = q - lax.rem(q, n_x) + lax.rem(lax.rem(q, n_x) + n_x - 1, n_x)
    w1_from = (aux, lax.rem(before - 2 + n_q, n_q) * 2 + side)

    barrier = pltpu.get_barrier_semaphore()

    def tell(device):
        pl.semaphore_signal(barrier, inc=1, device_id=device, device_id_type=MESH)

    for device in (along(-1), x2_from, w1_from, across, partner):
        tell(device)

    @pl.when(is_mid)
    def _():
        tell(at_z(end_of_mid))
        tell(at_z(other_mid))
        pl.semaphore_wait(barrier, 7)

    @pl.when(is_end)
    def _():
        tell(at_z(mid_of_end))
        pl.semaphore_wait(barrier, 6)

    def remote(src, dst, send, recv, device):
        return pltpu.make_async_remote_copy(src, dst, send, recv, device_id=device, device_id_type=MESH)

    def x1(c):
        return remote(own.at[c], vis.at[1, c], x1s.at[c], x1r.at[c], along(1))

    def w1(c):
        return remote(own.at[c], via.at[c], ws.at[c], wr.at[c], in_row(q + 2, 1))

    def x2(c):
        return remote(via.at[c], vis.at[3, c], x2s.at[c], x2r.at[c], in_row(q, n_x - 1))

    def z_own(c):
        return remote(own.at[c], vis.at[0, c], zs.at[c], zr.at[c], across)

    def z_vis(c):
        return remote(vis.at[1, c], vis.at[0, c], zs.at[c], zr.at[c], across)

    def x3(c):
        return remote(vis.at[0, c], vis.at[2, c], x3s.at[c], x3r.at[c], along(1))

    for c in range(chunks):
        x1(c).start()

        @pl.when(side == 0)
        def _():
            z_own(c).start()

    for c in range(chunks):
        w1(c).start()

    for c in range(chunks):
        high, low = split(own[c, :rows, :].T)
        own_th[pl.ds(c * LANES, LANES), :] = high
        own_tl[pl.ds(c * LANES, LANES), :] = low
        virt = own[c, pl.ds(rows + 1, 1), :]
        eps = own[c, pl.ds(rows, 1), :]
        row_e[pl.ds(c * LANES, LANES), :] = jnp.broadcast_to(virt - eps, (LANES, LANES)).T

    def visitor(d, c):
        return own.at[c] if d == 0 else vis.at[d - 1, c]

    def c1(u):
        d, c, n = UNITS[u]
        at = pl.ds(c, n)
        return remote(part.at[d, at, pl.ds(theirs, hw)], core_in.at[d, at], c1s.at[u], c1r.at[u], partner)

    def e(u):
        d, c, n = UNITS[u]
        at = pl.ds(c, n)
        return remote(half.at[d, at], end_in.at[d, at], es.at[u], er.at[u], at_z(mid_of_end))

    def m(u):
        d, c, n = UNITS[u]
        at = pl.ds(c, n)
        return remote(mid.at[d, at], mid_in.at[d, at], ms.at[u], mr.at[u], at_z(other_mid))

    def t(u):
        d, c, n = UNITS[u]
        block = amp.at[d, pl.ds(c, n), pl.ds(mine, hw)]
        return remote(block, block, ts.at[u], tr.at[u], at_z(end_of_mid))

    def c2(u):
        d, c, n = UNITS[u]
        block = amp.at[d, pl.ds(c, n), pl.ds(mine, hw)]
        return remote(block, block, c2s.at[u], c2r.at[u], partner)

    def joined(d, c, n):
        return jnp.concatenate([visitor(d, c + k)[:rows, :] for k in range(n)], axis=1)

    def stage_a(u):
        d, c, n = UNITS[u]
        for k in range(n):
            if d == 3:
                x3(c + k).wait_recv()
            if d == 4:
                x2(c + k).wait_recv()
            if d == 2:

                @pl.when(side == 0)
                def _():
                    x1(c + k).wait_recv()

        v_high, v_low = split(joined(d, c, n))

        @pl.loop(0, 2)
        def _(r):
            at = pl.ds(pl.multiple_of(r * hw, hw), hw)
            value = dot3(own_th[at, :], own_tl[at, :], v_high, v_low)
            for k in range(n):
                part[d, c + k, at, :] = value[:, k * LANES:(k + 1) * LANES]

        c1(u).start()

    def stage_b(u, middle):
        d, c, n = UNITS[u]
        c1(u).wait_recv()
        for k in range(n):
            half[d, c + k] = part[d, c + k, pl.ds(mine, hw), :] + core_in[d, c + k]
        if not middle:
            e(u).start()

    def stage_c(u, middle):
        d, c, n = UNITS[u]
        if middle:
            e(u).wait_recv()
            for k in range(n):
                mid[d, c + k] = half[d, c + k] + end_in[d, c + k]
            m(u).start()

    def stage_d(u, middle):
        d, c, n = UNITS[u]
        if middle:
            m(u).wait_recv()
            for k in range(n):
                total = mid[d, c + k] + mid_in[d, c + k]
                virt = own[c + k, pl.ds(rows + 1, 1), :]
                eps = visitor(d, c + k)[pl.ds(rows, 1), :]
                value = -total / (row_e[pl.ds(mine, hw), :] + (virt - eps))
                if d > 0:
                    live = own[c + k, pl.ds(rows + 1 + d, 1), :]
                    value = jnp.where(live > 0, value, jnp.zeros_like(value))
                amp[d, c + k, pl.ds(mine, hw), :] = value
            t(u).start()
        else:
            t(u).wait_recv()
        c2(u).start()

    def stage_e(u, first):
        d, c, n = UNITS[u]
        c2(u).wait_recv()
        t_high, t_low = split(jnp.concatenate([amp[d, c + k].T for k in range(n)], axis=0))
        step = rows // 4

        @pl.loop(0, 4)
        def _(r):
            at = pl.ds(pl.multiple_of(r * step, step), step)
            block = jnp.concatenate([visitor(d, c + k)[at, :] for k in range(n)], axis=1)
            v_high, v_low = split(block)
            value = dot3(v_high, v_low, t_high, t_low)
            if first:
                grad[at, :] = value
            else:
                grad[at, :] += value

    def stage_z(c):
        x1(c).wait_recv()
        z_vis(c).start()

    def stage_v(c):
        w1(c).wait_recv()
        x2(c).start()

    def stage_x(c):
        z_own(c).wait_recv()
        x3(c).start()

    def act(ops, middle):
        for op in ops:
            k = int(op[1:])
            if op[0] == "z":
                stage_z(k)
            elif op[0] == "v":
                stage_v(k)
            elif op[0] == "x":
                stage_x(k)
            else:
                {"B": stage_b, "C": stage_c, "D": stage_d}[op[0]](k, middle)

    kinds = [(side == 0) & is_end, (side == 0) & is_mid, (side == 1) & is_end, (side == 1) & is_mid]
    first = True
    for by_kind, common in PLAN:
        for kind, ops in enumerate(by_kind):
            if ops:
                pl.when(kinds[kind])(lambda ops=ops, kind=kind: act(ops, kind % 2 == 1))
        if common[:1] == "A":
            stage_a(int(common[1:]))
        if common[:1] == "E":
            stage_e(int(common[1:]), first)
            first = False

    for c in range(chunks):
        for copy in (x1, x2, z_own, x3, w1):
            copy(c).wait_send()
    for u in range(len(UNITS)):
        c1(u).wait_send()
        c2(u).wait_send()

        @pl.when(is_end)
        def _():
            e(u).wait_send()

        @pl.when(is_mid)
        def _():
            m(u).wait_send()
            t(u).wait_send()


def on_device(factors, eps_occ, eps_virt, pair_mask):
    rows, _, width = factors.shape
    chunks = width // LANES
    zl = lax.axis_size("aux") // 2
    n_q = lax.axis_size("occ") // 2
    group = lax.axis_index("occ")
    live = jnp.where(group >= jnp.arange(1, OFFSETS + 1), pair_mask[0], 0).astype(F32)
    blocks = factors.reshape(rows, chunks, LANES).transpose(1, 0, 2)
    extra = jnp.concatenate(
        [
            jnp.broadcast_to(eps_occ, (chunks, 1, LANES)),
            eps_virt.reshape(chunks, 1, LANES),
            jnp.broadcast_to(live[None, :, None], (chunks, OFFSETS, LANES)),
            jnp.zeros((chunks, PAD - 2 - OFFSETS, LANES), F32),
        ],
        axis=1,
    )
    own = jnp.concatenate([blocks, extra], axis=1)
    units, hw = len(UNITS), width // 2
    pairs = OFFSETS + 1
    dma = pltpu.SemaphoreType.DMA
    vmem = pltpu.VMEM
    sizes = (rows, width, chunks, zl, 4, n_q)
    grad = pl.pallas_call(
        lambda *refs: kernel(sizes, *refs),
        name="ri_mp2",
        out_shape=jax.ShapeDtypeStruct((rows, width), F32),
        in_specs=[pl.BlockSpec(memory_space=pltpu.VMEM)],
        out_specs=pl.BlockSpec(memory_space=pltpu.VMEM),
        scratch_shapes=[
            vmem((OFFSETS, chunks, rows + PAD, LANES), F32),
            vmem((width, rows), BF16),
            vmem((width, rows), BF16),
            vmem((width, LANES), F32),
            vmem((pairs, chunks, width, LANES), F32),
            vmem((pairs, chunks, hw, LANES), F32),
            vmem((pairs, chunks, hw, LANES), F32),
            vmem((pairs, chunks, hw, LANES), F32),
            vmem((pairs, chunks, hw, LANES), F32),
            vmem((pairs, chunks, hw, LANES), F32),
            vmem((pairs, chunks, width, LANES), F32),
            vmem((chunks, rows + PAD, LANES), F32),
        ]
        + [dma((chunks,))] * 10
        + [dma((units,))] * 10,
        compiler_params=pltpu.CompilerParams(
            collective_id=0, has_side_effects=True, vmem_limit_bytes=60 * 1024 * 1024
        ),
    )(own)
    return grad.reshape(factors.shape)


def solution(mesh):
    in_specs = (P("aux", "occ", None), P("occ"), P(), P("occ", None))
    out_specs = P("aux", "occ", None)
    return jax.shard_map(
        on_device, mesh=mesh, in_specs=in_specs, out_specs=out_specs, check_vma=False
    )
```

time: 424 us -> 222 us (0.52)
  the two profiles are of different devices: /device:TPU:2 before, /device:TPU:129 now
where the time goes in v1:
time: 222 us; the launch traced here: 221 us
  Pallas kernels  209 us (94%)
  local copies, waits for them, and re-layouts  10.6 us (5%)
    pallas_call x1, Pallas kernels, on_device(): pl.pallas_call(lambda *refs: kernel(sizes, *refs), name='ri_mp2', out_sha...  209 us
    reshape x1, local copies, waits for them, and re-layouts, on_device(): return grad.reshape(factors.shape)  5.07 us

profile of v1, /device:TPU:129, one launch (start us, length us, event | category | flops | bytes accessed | tf_op | source)
XLA Modules:
  0.0 221.4 jit_solution(3424581683273179778)
XLA Ops:
  0.7 0.7 fusion
  1.3 0.1 broadcast_in_dim.20
  1.4 0.0 copy-start
  1.4 1.7 copy.12
  3.1 0.0 copy-done
  3.2 3.7 %concatenate.3.refs_0_ = f32[4,1032,128]{2,1,0:T(8,128)} concatenate(f32[4,1024,128]{2,1,0:T(8,128)S(1)} %bitcast.10, f32[4,1,128]{2,1,0:T(1,128)S(1)} %broadcast_in_dim.18, f32[4,1,128]{2,1,0:T(1,128)S(1)} %bitcast.13, f32[4,4,128]{2,1,0:T(4,128)S(1)} %broadcast_in_dim.20, f32[4,2,128]{2,1,0:T(2,128)S(1)} %broadcast_in_dim.21), dimensions={1} | concatenate | bytes 4227072 | tf_op jit(solution)/shard_map/concatenate | solution.py:340
  6.9 209.5 %ri_mp2.1 = f32[1024,512]{1,0:T(8,128)} custom-call(f32[4,1032,128]{2,1,0:T(8,128)} %concatenate.3.refs_0_), custom_call_target="tpu_custom_call" | custom-call | tf_op jit(solution)/shard_map/ri_mp2/pallas_call | solution.py:346
  216.4 5.1 %copy.8 = f32[1024,1,512]{2,1,0:T(1,128)} copy(f32[1024,1,512]{2,0,1:T(8,128)} %bitcast.11) | data formatting | bytes 4194304 | tf_op jit(solution)/shard_map/reshape | solution.py:372
  (2 shorter events, 0.0 us)
Async XLA Ops:
  1.4 1.8 copy-start

commit v2 on v1

v2 whole, which is shorter than its diff:
```python
import jax
import jax.numpy as jnp
from jax import lax
from jax.experimental import pallas as pl
from jax.experimental.pallas import tpu as pltpu
from jax.sharding import PartitionSpec as P

OFFSETS = 4
LANES = 128
PAD = 8
MESH = pl.DeviceIdType.MESH
F32 = jnp.float32
BF16 = jnp.bfloat16

UNITS = [(0, 0, 1), (0, 1, 1), (0, 2, 1), (0, 3, 1), (2, 0, 2), (2, 2, 2), (4, 0, 1), (4, 1, 1), (4, 2, 1), (4, 3, 1), (1, 0, 2), (1, 2, 2), (3, 0, 1), (3, 1, 1), (3, 2, 1), (3, 3, 1)]
EARLY = 4
PLAN = [
    ([[], [], [], []], 'A1'),
    ([[], [], [], []], 'A0'),
    ([[], [], [], []], 'A2'),
    ([[], [], ['B1'], ['B1']], 'A3'),
    ([['v0'], ['v0'], ['z0', 'v0', 'z1'], ['C1', 'z0', 'v0', 'D1', 'z1']], 'A4'),
    ([['v1', 'v2', 'x0', 'B1'], ['v1', 'v2', 'x0', 'B1'], ['v1', 'x0', 'z2', 'v2', 'D1', 'z3'], ['v1', 'x0', 'z2', 'v2', 'z3']], 'A5'),
    ([['v3', 'B5', 'x1'], ['v3', 'B5', 'x1'], ['v3', 'x1'], ['v3', 'x1']], 'A10'),
    ([[], [], ['B5', 'B10'], ['B5', 'B10']], 'A12'),
    ([['B12'], ['B12'], [], []], 'A6'),
    ([['B6', 'B10'], ['B6', 'B10'], ['B12', 'B6'], ['B12', 'B6']], 'A7'),
    ([[], [], [], []], 'A13'),
    ([['B13'], ['B13'], ['x2', 'B4', 'B13'], ['x2', 'B4', 'B13']], 'A8'),
    ([['B8', 'x2', 'B3', 'B4'], ['B8', 'x2', 'B3', 'B4', 'C1', 'D1'], ['B8'], ['B8']], 'A14'),
    ([[], [], ['B14'], ['B14']], 'A9'),
    ([['B14', 'D1', 'x3', 'B0', 'B7', 'B9', 'B2'], ['B14', 'C5', 'C12', 'x3', 'B0', 'B7', 'B9', 'B2'], ['x3', 'B0', 'B7', 'B2', 'B3'], ['x3', 'B0', 'B7', 'B2', 'B3']], 'A11'),
    ([['B11'], ['C6', 'D5', 'B11', 'D12', 'C10', 'D6', 'C13'], ['B9', 'B11'], ['B9', 'B11']], 'A15'),
    ([['D5', 'B15'], [], ['B15', 'D5'], ['B15', 'C5', 'C10', 'D5', 'C12']], 'E5'),
    ([['D12', 'D6'], [], ['D10', 'D12'], ['C6', 'D10', 'D12', 'C4', 'D6']], 'E12'),
    ([[], [], ['D6'], ['C13']], 'E6'),
    ([['D10'], ['C8', 'B15', 'D10', 'C3'], [], []], 'E10'),
    ([['D13'], ['D13', 'D8'], ['D4', 'D13'], ['C8', 'D4', 'C14', 'C0', 'D13', 'C7', 'D8']], 'E13'),
    ([['D8'], ['C4'], ['D8'], ['C2']], 'E8'),
    ([['D3', 'D4', 'D0'], ['D3', 'C14', 'C0', 'C7', 'D4', 'C9'], [], []], 'E4'),
    ([['D14'], ['D0', 'D14', 'C2'], ['D0', 'D14'], ['D14', 'C3', 'D0']], 'E14'),
    ([['D7'], ['D7', 'C11', 'D9'], ['D7'], ['C9', 'D7']], 'E7'),
    ([['D9', 'D2'], ['D2', 'C15'], ['D2', 'D3'], ['D2', 'D3', 'C11']], 'E3'),
    ([[], [], ['D9'], ['D9', 'C15']], 'E9'),
    ([['D11'], ['D11'], ['D11'], ['D11']], 'E11'),
    ([['D15'], ['D15'], ['D15'], ['D15']], 'E15'),
]


def split(value):
    high = value.astype(BF16)
    return high, (value - high.astype(F32)).astype(BF16)


def dot3(a_high, a_low, b_high, b_low):
    def one(a, b):
        return lax.dot_general(a, b, (((1,), (0,)), ((), ())), preferred_element_type=F32)

    return one(a_high, b_high) + (one(a_high, b_low) + one(a_low, b_high))


def kernel(sizes, factors, eps_virt, eps_occ, mask, out, own, grad, vis, own_th, own_tl, row_e, part, core_in, half, end_in, mid, mid_in, amp, via, *sems):
    rows, width, chunks, zl, n_x, n_q = sizes
    (ws, wr, x1s, x1r, x2s, x2r, zs, zr, x3s, x3r, c1s, c1r, es, er, ms, mr, ts, tr, c2s, c2r) = sems
    hw = width // 2
    aux, occ = lax.axis_index("aux"), lax.axis_index("occ")
    core, z_lo = lax.rem(aux, 2), aux // 2
    side, q = lax.rem(occ, 2), occ // 2

    def along(k):
        return (aux, lax.rem(q + k + n_q, n_q) * 2 + side)

    def at_z(z):
        return (z * 2 + core, occ)

    across = (aux, q * 2 + 1 - side)
    partner = (z_lo * 2 + 1 - core, occ)
    low_half = z_lo < zl // 2
    is_mid = (z_lo == zl // 2 - 1) | (z_lo == zl // 2)
    is_end = jnp.logical_not(is_mid)
    mid_of_end = jnp.where(low_half, 1, zl - 2)
    end_of_mid = jnp.where(low_half, 0, zl - 1)
    other_mid = jnp.where(low_half, zl - 2, 1)

    def rows_of(u):
        d, c, n = UNITS[u]
        return (c + 1) * LANES if d == 0 else width

    def share(u, which):
        size = rows_of(u) // 2
        return pl.ds(pl.multiple_of(which * size, size), size)

    def mine(u):
        return share(u, core)

    def theirs(u):
        return share(u, 1 - core)

    def first_rows(u):
        return pl.ds(0, rows_of(u) // 2)

    def in_row(k, step):
        at = lax.rem(k + n_q, n_q)
        x_at = lax.rem(at, n_x)
        return (aux, (at - x_at + lax.rem(x_at + step, n_x)) * 2 + side)

    x2_from = in_row(q, 1)
    before = q - lax.rem(q, n_x) + lax.rem(lax.rem(q, n_x) + n_x - 1, n_x)
    w1_from = (aux, lax.rem(before - 2 + n_q, n_q) * 2 + side)

    barrier = pltpu.get_barrier_semaphore()

    def tell(device):
        pl.semaphore_signal(barrier, inc=1, device_id=device, device_id_type=MESH)

    for device in (along(-1), x2_from, w1_from, across, partner):
        tell(device)

    @pl.when(is_mid)
    def _():
        tell(at_z(end_of_mid))
        tell(at_z(other_mid))

    @pl.when(is_end)
    def _():
        tell(at_z(mid_of_end))

    eps = jnp.full((1, LANES), eps_occ[0], F32)
    live = [
        jnp.full((1, LANES), jnp.where(occ >= d, mask[0, d - 1], 0), jnp.int32).astype(F32)
        for d in range(1, OFFSETS + 1)
    ]
    blank = jnp.zeros((PAD - 2 - OFFSETS, LANES), F32)
    for c in range(chunks):
        own[c, pl.ds(0, rows), :] = factors[pl.ds(c, rows, stride=chunks), :]
        own[c, pl.ds(rows, PAD), :] = jnp.concatenate([eps, eps_virt[pl.ds(c, 1), :], *live, blank], axis=0)

    @pl.when(is_mid)
    def _():
        pl.semaphore_wait(barrier, 7)

    @pl.when(is_end)
    def _():
        pl.semaphore_wait(barrier, 6)

    def remote(src, dst, send, recv, device):
        return pltpu.make_async_remote_copy(src, dst, send, recv, device_id=device, device_id_type=MESH)

    def x1(c):
        return remote(own.at[c], vis.at[1, c], x1s.at[c], x1r.at[c], along(1))

    def w1(c):
        return remote(own.at[c], via.at[c], ws.at[c], wr.at[c], in_row(q + 2, 1))

    def x2(c):
        return remote(via.at[c], vis.at[3, c], x2s.at[c], x2r.at[c], in_row(q, n_x - 1))

    def z_own(c):
        return remote(own.at[c], vis.at[0, c], zs.at[c], zr.at[c], across)

    def z_vis(c):
        return remote(vis.at[1, c], vis.at[0, c], zs.at[c], zr.at[c], across)

    def x3(c):
        return remote(vis.at[0, c], vis.at[2, c], x3s.at[c], x3r.at[c], along(1))

    for c in range(chunks):
        x1(c).start()
        if c < EARLY:

            @pl.when(side == 0)
            def _():
                z_own(c).start()

    for c in range(chunks):
        w1(c).start()

    for c in range(chunks):
        high, low = split(own[c, :rows, :].T)
        own_th[pl.ds(c * LANES, LANES), :] = high
        own_tl[pl.ds(c * LANES, LANES), :] = low
        virt = own[c, pl.ds(rows + 1, 1), :]
        eps = own[c, pl.ds(rows, 1), :]
        row_e[pl.ds(c * LANES, LANES), :] = jnp.broadcast_to(virt - eps, (LANES, LANES)).T

    def visitor(d, c):
        return own.at[c] if d == 0 else vis.at[d - 1, c]

    def c1(u):
        d, c, n = UNITS[u]
        at = pl.ds(c, n)
        return remote(part.at[d, at, theirs(u)], core_in.at[d, at, first_rows(u)], c1s.at[u], c1r.at[u], partner)

    def e(u):
        d, c, n = UNITS[u]
        at = pl.ds(c, n)
        return remote(half.at[d, at, first_rows(u)], end_in.at[d, at, first_rows(u)], es.at[u], er.at[u], at_z(mid_of_end))

    def m(u):
        d, c, n = UNITS[u]
        at = pl.ds(c, n)
        return remote(mid.at[d, at, first_rows(u)], mid_in.at[d, at, first_rows(u)], ms.at[u], mr.at[u], at_z(other_mid))

    def t(u):
        d, c, n = UNITS[u]
        block = amp.at[d, pl.ds(c, n), mine(u)]
        return remote(block, block, ts.at[u], tr.at[u], at_z(end_of_mid))

    def c2(u):
        d, c, n = UNITS[u]
        block = amp.at[d, pl.ds(c, n), mine(u)]
        return remote(block, block, c2s.at[u], c2r.at[u], partner)

    def joined(d, c, n):
        return jnp.concatenate([visitor(d, c + k)[:rows, :] for k in range(n)], axis=1)

    def stage_a(u):
        d, c, n = UNITS[u]
        for k in range(n):
            if d == 3:
                x3(c + k).wait_recv()
            if d == 4:
                x2(c + k).wait_recv()
            if d == 2:

                @pl.when(side == 0)
                def _():
                    x1(c + k).wait_recv()

        v_high, v_low = split(joined(d, c, n))

        at = pl.ds(0, rows_of(u))
        value = dot3(own_th[at, :], own_tl[at, :], v_high, v_low)
        for k in range(n):
            part[d, c + k, at, :] = value[:, k * LANES:(k + 1) * LANES]
        c1(u).start()

    def stage_b(u, middle):
        d, c, n = UNITS[u]
        c1(u).wait_recv()
        for k in range(n):
            half[d, c + k, first_rows(u), :] = part[d, c + k, mine(u), :] + core_in[d, c + k, first_rows(u), :]
        if not middle:
            e(u).start()

    def stage_c(u, middle):
        d, c, n = UNITS[u]
        if middle:
            e(u).wait_recv()
            for k in range(n):
                mid[d, c + k, first_rows(u), :] = half[d, c + k, first_rows(u), :] + end_in[d, c + k, first_rows(u), :]
            m(u).start()

    def stage_d(u, middle):
        d, c, n = UNITS[u]
        if middle:
            m(u).wait_recv()
            for k in range(n):
                total = mid[d, c + k, first_rows(u), :] + mid_in[d, c + k, first_rows(u), :]
                virt = own[c + k, pl.ds(rows + 1, 1), :]
                eps = visitor(d, c + k)[pl.ds(rows, 1), :]
                value = -total / (row_e[mine(u), :] + (virt - eps))
                if d > 0:
                    live = own[c + k, pl.ds(rows + 1 + d, 1), :]
                    value = jnp.where(live > 0, value, jnp.zeros_like(value))
                amp[d, c + k, mine(u), :] = value
            t(u).start()
        else:
            t(u).wait_recv()
        c2(u).start()

    def transposed(d, c):
        if d > 0:
            return amp[d, c].T
        blocks = [
            amp[0, c, pl.ds(r * LANES, LANES), :].T if r <= c else amp[0, r, pl.ds(c * LANES, LANES), :]
            for r in range(chunks)
        ]
        return jnp.concatenate(blocks, axis=1)

    def stage_e(u, first, last):
        d, c, n = UNITS[u]
        if d == 0:
            for k in range(u + 1):
                c2(k).wait_recv()
            c, n = 0, chunks
        else:
            c2(u).wait_recv()
        t_high, t_low = split(jnp.concatenate([transposed(d, c + k) for k in range(n)], axis=0))
        steps = 2
        step = rows // steps

        def contracted(at):
            block = jnp.concatenate([visitor(d, c + k)[at, :] for k in range(n)], axis=1)
            v_high, v_low = split(block)
            value = dot3(v_high, v_low, t_high, t_low)
            return value if first else grad[at, :] + value

        if last:
            for r in range(steps):
                value = contracted(pl.ds(r * step, step))
                for k in range(chunks):
                    out[pl.ds(r * step * chunks + k, step, stride=chunks), :] = value[:, k * LANES:(k + 1) * LANES]
        else:

            @pl.loop(0, steps)
            def _(r):
                at = pl.ds(pl.multiple_of(r * step, step), step)
                grad[at, :] = contracted(at)

    def stage_z(c):
        x1(c).wait_recv()
        z_vis(c).start()

    def stage_v(c):
        w1(c).wait_recv()
        x2(c).start()

    def stage_x(c):
        z_own(c).wait_recv()
        x3(c).start()

    def act(ops, middle):
        for op in ops:
            k = int(op[1:])
            if op[0] == "y":
                z_own(k).start()
            elif op[0] == "z":
                stage_z(k)
            elif op[0] == "v":
                stage_v(k)
            elif op[0] == "x":
                stage_x(k)
            else:
                {"B": stage_b, "C": stage_c, "D": stage_d}[op[0]](k, middle)

    kinds = [(side == 0) & is_end, (side == 0) & is_mid, (side == 1) & is_end, (side == 1) & is_mid]
    order = [common for _, common in PLAN if common[:1] == "E"]
    for by_kind, common in PLAN:
        for kind, ops in enumerate(by_kind):
            if ops:
                pl.when(kinds[kind])(lambda ops=ops, kind=kind: act(ops, kind % 2 == 1))
        if common[:1] == "A":
            stage_a(int(common[1:]))
        if common[:1] == "E":
            stage_e(int(common[1:]), common == order[0], common == order[-1])

    for c in range(chunks):
        for copy in (x1, x2, z_own, x3, w1):
            copy(c).wait_send()
    for u in range(len(UNITS)):
        c1(u).wait_send()
        c2(u).wait_send()

        @pl.when(is_end)
        def _():
            e(u).wait_send()

        @pl.when(is_mid)
        def _():
            m(u).wait_send()
            t(u).wait_send()


def write_out(source, result, done):
    step = source.shape[0] // done.shape[0]
    copies = []
    for k in range(done.shape[0]):
        at = pl.ds(k * step, step)
        copies.append(pltpu.make_async_copy(source.at[at], result.at[at], done.at[k]))
    for copy in copies:
        copy.start()
    for copy in copies:
        copy.wait()


def on_device(factors, eps_occ, eps_virt, pair_mask):
    rows, _, width = factors.shape
    chunks = width // LANES
    zl = lax.axis_size("aux") // 2
    n_q = lax.axis_size("occ") // 2
    units, hw = len(UNITS), width // 2
    pairs = OFFSETS + 1
    dma = pltpu.SemaphoreType.DMA
    vmem = pltpu.VMEM
    sizes = (rows, width, chunks, zl, 4, n_q)
    in_vmem = pl.BlockSpec(memory_space=pltpu.VMEM)
    in_smem = pl.BlockSpec(memory_space=pltpu.SMEM)
    grad = pl.pallas_call(
        lambda *refs: kernel(sizes, *refs),
        name="ri_mp2",
        out_shape=jax.ShapeDtypeStruct((rows * chunks, LANES), F32),
        in_specs=[in_vmem, in_vmem, in_smem, in_smem],
        out_specs=in_vmem,
        scratch_shapes=[
            vmem((chunks, rows + PAD, LANES), F32),
            vmem((rows, width), F32),
            vmem((OFFSETS, chunks, rows + PAD, LANES), F32),
            vmem((width, rows), BF16),
            vmem((width, rows), BF16),
            vmem((width, LANES), F32),
            vmem((pairs, chunks, width, LANES), F32),
            vmem((pairs, chunks, hw, LANES), F32),
            vmem((pairs, chunks, hw, LANES), F32),
            vmem((pairs, chunks, hw, LANES), F32),
            vmem((pairs, chunks, hw, LANES), F32),
            vmem((pairs, chunks, hw, LANES), F32),
            vmem((pairs, chunks, width, LANES), F32),
            vmem((chunks, rows + PAD, LANES), F32),
        ]
        + [dma((chunks,))] * 10
        + [dma((units,))] * 10,
        compiler_params=pltpu.CompilerParams(
            collective_id=0, has_side_effects=True, vmem_limit_bytes=60 * 1024 * 1024
        ),
    )(factors.reshape(rows * chunks, LANES), eps_virt.reshape(chunks, LANES), eps_occ, pair_mask)
    result = pl.pallas_call(
        write_out,
        name="write_out",
        out_shape=jax.ShapeDtypeStruct(grad.shape, F32),
        in_specs=[in_vmem],
        out_specs=pl.BlockSpec(memory_space=pl.ANY),
        scratch_shapes=[dma((8,))],
    )(grad)
    return result.reshape(factors.shape)


def solution(mesh):
    in_specs = (P("aux", "occ", None), P("occ"), P(), P("occ", None))
    out_specs = P("aux", "occ", None)
    return jax.shard_map(
        on_device, mesh=mesh, in_specs=in_specs, out_specs=out_specs, check_vma=False
    )
```

time: 222 us -> 195 us (0.88)
  the two profiles are of different devices: /device:TPU:129 before, /device:TPU:2 now
where the time goes in v2:
time: 195 us; the launch traced here: 192 us
  Pallas kernels  191 us (98%)
    pallas_call x1, Pallas kernels, on_device(): pl.pallas_call(lambda *refs: kernel(sizes, *refs), name='ri_mp2', out_sha...  188 us

profile of v2, /device:TPU:2, one launch (start us, length us, event | category | flops | bytes accessed | tf_op | source)
XLA Modules:
  0.0 191.9 jit_solution(5516742901091609753)
XLA Ops:
  0.7 188.1 %ri_mp2.1.source = f32[4096,128]{1,0:T(8,128)} custom-call(f32[4096,128]{1,0:T(8,128)} %bitcast.3, f32[4,128]{1,0:T(4,128)} %bitcast.4, f32[1]{0:T(128)S(6)} %copy.6.refs_2_, s32[1,4]{1,0:T(1,128)} %refs_3_.1), custom_call_target="tpu_custom_call" | custom-call | tf_op jit(solution)/shard_map/ri_mp2/pallas_call | solution.py:389
  188.7 3.0 %write_out.1 = f32[4096,128]{1,0:T(8,128)} custom-call(f32[4096,128]{1,0:T(8,128)} %ri_mp2.1.source), custom_call_target="tpu_custom_call" | custom-call | tf_op jit(solution)/shard_map/write_out/pallas_call | solution.py:417

commit v3 on v2

--- a/solution.py
+++ b/solution.py
@@ -8,43 +8,57 @@
 OFFSETS = 4
 LANES = 128
 PAD = 8
+VMEM_MIB = 48
 MESH = pl.DeviceIdType.MESH
 F32 = jnp.float32
 BF16 = jnp.bfloat16
 
-UNITS = [(0, 0, 1), (0, 1, 1), (0, 2, 1), (0, 3, 1), (2, 0, 2), (2, 2, 2), (4, 0, 1), (4, 1, 1), (4, 2, 1), (4, 3, 1), (1, 0, 2), (1, 2, 2), (3, 0, 1), (3, 1, 1), (3, 2, 1), (3, 3, 1)]
-EARLY = 4
+UNITS = [(0, 0, 1, 0, 128), (0, 1, 1, 0, 256), (0, 2, 1, 0, 384), (0, 3, 1, 0, 512), (2, 0, 1, 0, 512), (2, 1, 1, 0, 512), (2, 2, 1, 0, 256), (2, 2, 1, 256, 512), (2, 3, 1, 0, 256), (2, 3, 1, 256, 512), (4, 0, 1, 0, 512), (4, 1, 1, 0, 512), (4, 2, 1, 0, 256), (4, 2, 1, 256, 512), (4, 3, 1, 0, 256), (4, 3, 1, 256, 512), (1, 0, 2, 0, 512), (1, 2, 1, 0, 512), (1, 3, 1, 0, 512), (3, 0, 1, 0, 512), (3, 1, 1, 0, 512), (3, 2, 1, 0, 512), (3, 3, 1, 0, 256), (3, 3, 1, 256, 512)]
+EARLY = 6
 PLAN = [
+    ([[], [], [], []], 'A2'),
     ([[], [], [], []], 'A1'),
+    ([[], [], [], []], 'A3'),
     ([[], [], [], []], 'A0'),
-    ([[], [], [], []], 'A2'),
-    ([[], [], ['B1'], ['B1']], 'A3'),
-    ([['v0'], ['v0'], ['z0', 'v0', 'z1'], ['C1', 'z0', 'v0', 'D1', 'z1']], 'A4'),
-    ([['v1', 'v2', 'x0', 'B1'], ['v1', 'v2', 'x0', 'B1'], ['v1', 'x0', 'z2', 'v2', 'D1', 'z3'], ['v1', 'x0', 'z2', 'v2', 'z3']], 'A5'),
-    ([['v3', 'B5', 'x1'], ['v3', 'B5', 'x1'], ['v3', 'x1'], ['v3', 'x1']], 'A10'),
-    ([[], [], ['B5', 'B10'], ['B5', 'B10']], 'A12'),
-    ([['B12'], ['B12'], [], []], 'A6'),
-    ([['B6', 'B10'], ['B6', 'B10'], ['B12', 'B6'], ['B12', 'B6']], 'A7'),
+    ([['B0'], ['B0'], ['z0', 'z1', 'z2'], ['z0', 'z1', 'z2']], 'A4'),
+    ([['v0'], ['v0'], ['v0', 'z3'], ['v0', 'z3']], 'A5'),
+    ([['v1', 'x0'], ['v1', 'x0'], ['v1', 'x0', 'z4'], ['v1', 'x0', 'z4']], 'A6'),
+    ([['v2'], ['v2'], ['v2'], ['v2']], 'A7'),
+    ([[], [], ['z5'], ['z5']], 'A8'),
+    ([['v3'], ['v3'], ['v3'], ['v3']], 'A9'),
+    ([['x1', 'B2'], ['x1', 'B2'], ['x1', 'B2'], ['x1', 'B2']], 'A16'),
+    ([['B16'], ['B16'], ['B16'], ['B16']], 'A19'),
+    ([[], [], [], []], 'A10'),
+    ([['B19'], ['B19'], ['B19'], ['B19']], 'A20'),
+    ([[], [], [], []], 'A11'),
+    ([['B20', 'B11', 'x2', 'B1', 'B3'], ['B20', 'B11', 'x2', 'B1', 'B3'], ['x2', 'B1', 'B3', 'B0', 'B20'], ['x2', 'B1', 'B3', 'B0', 'B20']], 'A17'),
+    ([['B17'], ['B17'], ['B11', 'B17'], ['B11', 'B17']], 'A12'),
     ([[], [], [], []], 'A13'),
-    ([['B13'], ['B13'], ['x2', 'B4', 'B13'], ['x2', 'B4', 'B13']], 'A8'),
-    ([['B8', 'x2', 'B3', 'B4'], ['B8', 'x2', 'B3', 'B4', 'C1', 'D1'], ['B8'], ['B8']], 'A14'),
-    ([[], [], ['B14'], ['B14']], 'A9'),
-    ([['B14', 'D1', 'x3', 'B0', 'B7', 'B9', 'B2'], ['B14', 'C5', 'C12', 'x3', 'B0', 'B7', 'B9', 'B2'], ['x3', 'B0', 'B7', 'B2', 'B3'], ['x3', 'B0', 'B7', 'B2', 'B3']], 'A11'),
-    ([['B11'], ['C6', 'D5', 'B11', 'D12', 'C10', 'D6', 'C13'], ['B9', 'B11'], ['B9', 'B11']], 'A15'),
-    ([['D5', 'B15'], [], ['B15', 'D5'], ['B15', 'C5', 'C10', 'D5', 'C12']], 'E5'),
-    ([['D12', 'D6'], [], ['D10', 'D12'], ['C6', 'D10', 'D12', 'C4', 'D6']], 'E12'),
-    ([[], [], ['D6'], ['C13']], 'E6'),
-    ([['D10'], ['C8', 'B15', 'D10', 'C3'], [], []], 'E10'),
-    ([['D13'], ['D13', 'D8'], ['D4', 'D13'], ['C8', 'D4', 'C14', 'C0', 'D13', 'C7', 'D8']], 'E13'),
-    ([['D8'], ['C4'], ['D8'], ['C2']], 'E8'),
-    ([['D3', 'D4', 'D0'], ['D3', 'C14', 'C0', 'C7', 'D4', 'C9'], [], []], 'E4'),
-    ([['D14'], ['D0', 'D14', 'C2'], ['D0', 'D14'], ['D14', 'C3', 'D0']], 'E14'),
-    ([['D7'], ['D7', 'C11', 'D9'], ['D7'], ['C9', 'D7']], 'E7'),
-    ([['D9', 'D2'], ['D2', 'C15'], ['D2', 'D3'], ['D2', 'D3', 'C11']], 'E3'),
-    ([[], [], ['D9'], ['D9', 'C15']], 'E9'),
-    ([['D11'], ['D11'], ['D11'], ['D11']], 'E11'),
-    ([['D15'], ['D15'], ['D15'], ['D15']], 'E15'),
+    ([['B12', 'B13'], ['B12', 'B13'], ['B12', 'B13'], ['B12', 'B13']], 'A21'),
+    ([['B21'], ['B21'], ['B21'], ['B21']], 'A14'),
+    ([[], [], [], []], 'A15'),
+    ([['x3', 'B10', 'B6', 'B7', 'D0', 'B5', 'B8', 'B9', 'B4', 'B14', 'B15'], ['C0', 'D0', 'C2', 'x3', 'B10', 'B6', 'B7', 'B5', 'B8', 'B9', 'B4', 'B14', 'B15'], ['B14', 'x3', 'B10', 'B6', 'B7', 'B5', 'B8', 'B9', 'B4', 'B15'], ['B14', 'x3', 'B10', 'B6', 'B7', 'B5', 'B8', 'B9', 'B4', 'B15']], 'A18'),
+    ([['B18', 'D2'], ['D2', 'B18', 'C16', 'C19', 'C20', 'D16', 'C11'], ['B18', 'D2'], ['B18', 'C2', 'D2', 'C16']], 'A22'),
+    ([[], [], [], ['C19']], 'A23'),
+    ([['B22', 'B23', 'D16'], ['C1'], ['B22', 'B23', 'D16'], ['C1', 'B22', 'B23', 'C3', 'D16', 'C0']], 'E16'),
+    ([['D19'], ['D19', 'B22', 'B23', 'C3', 'D20'], ['D19', 'D1'], ['D19', 'D1', 'C20']], 'E19'),
+    ([['D20'], [], ['D3', 'D0', 'D20'], ['D3', 'C11', 'D0', 'C17', 'D20', 'C12', 'C13']], 'E20'),
+    ([['D11', 'D1', 'D3'], ['D11', 'C17', 'C12', 'D1', 'C13', 'D3', 'C21'], [], []], 'E3'),
+    ([[], [], ['D11'], ['D11', 'C21', 'C14', 'D17']], 'E11'),
+    ([['D17', 'D12'], ['D17', 'D12', 'C10', 'C6', 'D13'], ['D17', 'D12'], ['D12']], 'E17'),
+    ([['D13'], ['C7'], ['D13'], ['D13', 'C10', 'C6']], 'E13'),
+    ([['D21'], ['D21', 'C5'], ['D21', 'D14'], ['D21', 'C7', 'D14']], 'E21'),
+    ([['D10', 'D6'], ['D10', 'C8', 'C9', 'D6'], ['D10', 'D6'], ['C5', 'C8', 'D10', 'C9', 'D6']], 'E10'),
+    ([['D7'], ['D7', 'C4'], ['D7'], ['D7', 'C4']], 'E7'),
+    ([['D5', 'D8'], ['D5', 'C14', 'C15', 'D8'], ['D5', 'D8'], ['D5', 'C15', 'D8']], 'E5'),
+    ([['D9'], ['D9', 'C18'], ['D9'], ['D9', 'C18', 'C22']], 'E9'),
+    ([['D4', 'D14'], ['D4', 'C22', 'C23', 'D14'], ['D4', 'D15'], ['D4', 'C23', 'D15']], 'E4'),
+    ([['D15'], ['D15'], [], []], 'E15'),
+    ([['D18', 'D22'], ['D18', 'D22'], ['D18', 'D22'], ['D18', 'D22']], 'E18'),
+    ([['D23'], ['D23'], ['D23'], ['D23']], 'E23'),
 ]
+
+PIECES = [(0, 0, 256), (0, 256, 256), (0, 512, 512 + PAD), (1, 0, 1024), (2, 0, 1024), (3, 0, 1024)]
 
 
 def split(value):
@@ -83,12 +97,11 @@
     other_mid = jnp.where(low_half, zl - 2, 1)
 
     def rows_of(u):
-        d, c, n = UNITS[u]
-        return (c + 1) * LANES if d == 0 else width
+        return UNITS[u][4] - UNITS[u][3]
 
     def share(u, which):
         size = rows_of(u) // 2
-        return pl.ds(pl.multiple_of(which * size, size), size)
+        return pl.ds(pl.multiple_of(UNITS[u][3] + which * size, size), size)
 
     def mine(u):
         return share(u, core)
@@ -97,7 +110,7 @@
         return share(u, 1 - core)
 
     def first_rows(u):
-        return pl.ds(0, rows_of(u) // 2)
+        return pl.ds(UNITS[u][3] // 2, rows_of(u) // 2)
 
     def in_row(k, step):
         at = lax.rem(k + n_q, n_q)
@@ -146,33 +159,47 @@
     def remote(src, dst, send, recv, device):
         return pltpu.make_async_remote_copy(src, dst, send, recv, device_id=device, device_id_type=MESH)
 
-    def x1(c):
-        return remote(own.at[c], vis.at[1, c], x1s.at[c], x1r.at[c], along(1))
+    def full(c):
+        return pl.ds(0, rows + PAD if c == 0 else rows)
+
+    def piece(ref, p, *slot):
+        c, row, size = PIECES[p]
+        return ref.at[(*slot, c, pl.ds(row, size))]
+
+    def pieces_of(c):
+        return [p for p, item in enumerate(PIECES) if item[0] == c]
+
+    def x1(p):
+        return remote(piece(own, p), piece(vis, p, 1), x1s.at[p], x1r.at[p], along(1))
 
     def w1(c):
-        return remote(own.at[c], via.at[c], ws.at[c], wr.at[c], in_row(q + 2, 1))
+        return remote(own.at[c, full(c)], via.at[c, full(c)], ws.at[c], wr.at[c], in_row(q + 2, 1))
 
     def x2(c):
-        return remote(via.at[c], vis.at[3, c], x2s.at[c], x2r.at[c], in_row(q, n_x - 1))
-
-    def z_own(c):
-        return remote(own.at[c], vis.at[0, c], zs.at[c], zr.at[c], across)
-
-    def z_vis(c):
-        return remote(vis.at[1, c], vis.at[0, c], zs.at[c], zr.at[c], across)
+        return remote(via.at[c, full(c)], vis.at[3, c, full(c)], x2s.at[c], x2r.at[c], in_row(q, n_x - 1))
+
+    def z_own(p):
+        return remote(piece(own, p), piece(vis, p, 0), zs.at[p], zr.at[p], across)
+
+    def z_vis(p):
+        return remote(piece(vis, p, 1), piece(vis, p, 0), zs.at[p], zr.at[p], across)
 
     def x3(c):
-        return remote(vis.at[0, c], vis.at[2, c], x3s.at[c], x3r.at[c], along(1))
-
-    for c in range(chunks):
-        x1(c).start()
-        if c < EARLY:
+        return remote(vis.at[0, c, full(c)], vis.at[2, c, full(c)], x3s.at[c], x3r.at[c], along(1))
+
+    def first_hop(p):
+        x1(p).start()
+        if p < EARLY:
 
             @pl.when(side == 0)
             def _():
-                z_own(c).start()
-
-    for c in range(chunks):
+                z_own(p).start()
+
+    for p in range(len(PIECES)):
+        if p == 4:
+            w1(0).start()
+        first_hop(p)
+    for c in range(1, chunks):
         w1(c).start()
 
     for c in range(chunks):
@@ -187,56 +214,62 @@
         return own.at[c] if d == 0 else vis.at[d - 1, c]
 
     def c1(u):
-        d, c, n = UNITS[u]
+        d, c, n = UNITS[u][:3]
         at = pl.ds(c, n)
         return remote(part.at[d, at, theirs(u)], core_in.at[d, at, first_rows(u)], c1s.at[u], c1r.at[u], partner)
 
     def e(u):
-        d, c, n = UNITS[u]
+        d, c, n = UNITS[u][:3]
         at = pl.ds(c, n)
         return remote(half.at[d, at, first_rows(u)], end_in.at[d, at, first_rows(u)], es.at[u], er.at[u], at_z(mid_of_end))
 
     def m(u):
-        d, c, n = UNITS[u]
+        d, c, n = UNITS[u][:3]
         at = pl.ds(c, n)
         return remote(mid.at[d, at, first_rows(u)], mid_in.at[d, at, first_rows(u)], ms.at[u], mr.at[u], at_z(other_mid))
 
     def t(u):
-        d, c, n = UNITS[u]
+        d, c, n = UNITS[u][:3]
         block = amp.at[d, pl.ds(c, n), mine(u)]
         return remote(block, block, ts.at[u], tr.at[u], at_z(end_of_mid))
 
     def c2(u):
-        d, c, n = UNITS[u]
+        d, c, n = UNITS[u][:3]
         block = amp.at[d, pl.ds(c, n), mine(u)]
         return remote(block, block, c2s.at[u], c2r.at[u], partner)
 
     def joined(d, c, n):
         return jnp.concatenate([visitor(d, c + k)[:rows, :] for k in range(n)], axis=1)
 
+    arrived = set()
+
     def stage_a(u):
-        d, c, n = UNITS[u]
-        for k in range(n):
+        d, c, n = UNITS[u][:3]
+        for k in range(c, c + n):
+            if (d, k) in arrived:
+                continue
+            arrived.add((d, k))
             if d == 3:
-                x3(c + k).wait_recv()
+                x3(k).wait_recv()
             if d == 4:
-                x2(c + k).wait_recv()
+                x2(k).wait_recv()
             if d == 2:
 
                 @pl.when(side == 0)
                 def _():
-                    x1(c + k).wait_recv()
+                    for p in pieces_of(k):
+                        x1(p).wait_recv()
 
         v_high, v_low = split(joined(d, c, n))
 
-        at = pl.ds(0, rows_of(u))
+        at = pl.ds(UNITS[u][3], rows_of(u))
         value = dot3(own_th[at, :], own_tl[at, :], v_high, v_low)
         for k in range(n):
             part[d, c + k, at, :] = value[:, k * LANES:(k + 1) * LANES]
         c1(u).start()
 
     def stage_b(u, middle):
-        d, c, n = UNITS[u]
+        d, c, n = UNITS[u][:3]
         c1(u).wait_recv()
         for k in range(n):
             half[d, c + k, first_rows(u), :] = part[d, c + k, mine(u), :] + core_in[d, c + k, first_rows(u), :]
@@ -244,7 +277,7 @@
             e(u).start()
 
     def stage_c(u, middle):
-        d, c, n = UNITS[u]
+        d, c, n = UNITS[u][:3]
         if middle:
             e(u).wait_recv()
             for k in range(n):
@@ -252,13 +285,13 @@
             m(u).start()
 
     def stage_d(u, middle):
-        d, c, n = UNITS[u]
+        d, c, n = UNITS[u][:3]
         if middle:
             m(u).wait_recv()
             for k in range(n):
                 total = mid[d, c + k, first_rows(u), :] + mid_in[d, c + k, first_rows(u), :]
                 virt = own[c + k, pl.ds(rows + 1, 1), :]
-                eps = visitor(d, c + k)[pl.ds(rows, 1), :]
+                eps = visitor(d, 0)[pl.ds(rows, 1), :]
                 value = -total / (row_e[mine(u), :] + (virt - eps))
                 if d > 0:
                     live = own[c + k, pl.ds(rows + 1 + d, 1), :]
@@ -279,13 +312,12 @@
         return jnp.concatenate(blocks, axis=1)
 
     def stage_e(u, first, last):
-        d, c, n = UNITS[u]
+        d, c, n = UNITS[u][:3]
+        for k, other in enumerate(UNITS):
+            if other[0] == d and (d == 0 or other[1] == c):
+                c2(k).wait_recv()
         if d == 0:
-            for k in range(u + 1):
-                c2(k).wait_recv()
             c, n = 0, chunks
-        else:
-            c2(u).wait_recv()
         t_high, t_low = split(jnp.concatenate([transposed(d, c + k) for k in range(n)], axis=0))
         steps = 2
         step = rows // steps
@@ -317,7 +349,8 @@
         x2(c).start()
 
     def stage_x(c):
-        z_own(c).wait_recv()
+        for p in pieces_of(c):
+            z_own(p).wait_recv()
         x3(c).start()
 
     def act(ops, middle):
@@ -346,8 +379,11 @@
             stage_e(int(common[1:]), common == order[0], common == order[-1])
 
     for c in range(chunks):
-        for copy in (x1, x2, z_own, x3, w1):
+        for copy in (x2, x3, w1):
             copy(c).wait_send()
+    for p in range(len(PIECES)):
+        x1(p).wait_send()
+        z_own(p).wait_send()
     for u in range(len(UNITS)):
         c1(u).wait_send()
         c2(u).wait_send()
@@ -408,19 +444,20 @@
             vmem((pairs, chunks, width, LANES), F32),
             vmem((chunks, rows + PAD, LANES), F32),
         ]
-        + [dma((chunks,))] * 10
+        + [dma((len(PIECES),))] * 10
         + [dma((units,))] * 10,
         compiler_params=pltpu.CompilerParams(
-            collective_id=0, has_side_effects=True, vmem_limit_bytes=60 * 1024 * 1024
+            collective_id=0, has_side_effects=True, vmem_limit_bytes=VMEM_MIB * 1024 * 1024
         ),
     )(factors.reshape(rows * chunks, LANES), eps_virt.reshape(chunks, LANES), eps_occ, pair_mask)
     result = pl.pallas_call(
         write_out,
         name="write_out",
         out_shape=jax.ShapeDtypeStruct(grad.shape, F32),
-        in_specs=[in_vmem],
-        out_specs=pl.BlockSpec(memory_space=pl.ANY),
+        in_specs=[pl.BlockSpec(memory_space=pl.ANY)],
+        out_specs=pl.BlockSpec(memory_space=pltpu.HBM),
         scratch_shapes=[dma((8,))],
+        compiler_params=pltpu.CompilerParams(vmem_limit_bytes=1024 * 1024),
     )(grad)
     return result.reshape(factors.shape)
 

time: 195 us -> 183 us (0.938); the launches traced: 192 us -> 183 us
  Pallas kernels: 191 us -> 179 us
  local copies, waits for them, and re-layouts: 0 us -> 2.92 us
    pallas_call x1, Pallas kernels: 188 us -> 178 us  [on_device(): pl.pallas_call(lambda *refs: kernel(sizes, *refs), name='ri_mp2', out_sha...]
    unnamed x0 -> x6, local copies, waits for them, and re-layouts: none -> 2.92 us
where the time goes in v3:
time: 183 us
  Pallas kernels  179 us (98%)
  local copies, waits for them, and re-layouts  2.92 us (2%)
    pallas_call x1, Pallas kernels, on_device(): pl.pallas_call(lambda *refs: kernel(sizes, *refs), name='ri_mp2', out_sha...  178 us

profile of v3, /device:TPU:2, one launch (start us, length us, event | category | flops | bytes accessed | tf_op | source)
XLA Modules:
  0.0 182.7 jit_solution(11491961917966454367)
XLA Ops:
  0.7 0.0 copy-start
  0.7 1.6 copy-done
  2.2 0.0 copy-start.1
  2.2 0.7 copy-done.1
  2.9 0.0 copy-start.2
  2.9 0.7 copy-done.2
  3.6 177.6 %ri_mp2.1.source = f32[4096,128]{1,0:T(8,128)S(1)} custom-call(f32[4096,128]{1,0:T(8,128)S(1)} %bitcast.3, f32[4,128]{1,0:T(4,128)S(1)} %bitcast.4, f32[1]{0:T(128)S(6)} %copy.6.refs_2_, s32[1,4]{1,0:T(1,128)S(1)} %copy-done.2), custom_call_target="tpu_custom_call" | custom-call | tf_op jit(solution)/shard_map/ri_mp2/pallas_call | solution.py:425
  181.2 1.4 write_out.1
Async XLA Ops:
  0.7 1.6 copy-start
  2.2 0.7 copy-start.1
  2.9 0.7 copy-start.2

commit v4 on v3

--- a/solution.py
+++ b/solution.py
@@ -14,51 +14,51 @@
 BF16 = jnp.bfloat16
 
 UNITS = [(0, 0, 1, 0, 128), (0, 1, 1, 0, 256), (0, 2, 1, 0, 384), (0, 3, 1, 0, 512), (2, 0, 1, 0, 512), (2, 1, 1, 0, 512), (2, 2, 1, 0, 256), (2, 2, 1, 256, 512), (2, 3, 1, 0, 256), (2, 3, 1, 256, 512), (4, 0, 1, 0, 512), (4, 1, 1, 0, 512), (4, 2, 1, 0, 256), (4, 2, 1, 256, 512), (4, 3, 1, 0, 256), (4, 3, 1, 256, 512), (1, 0, 2, 0, 512), (1, 2, 1, 0, 512), (1, 3, 1, 0, 512), (3, 0, 1, 0, 512), (3, 1, 1, 0, 512), (3, 2, 1, 0, 512), (3, 3, 1, 0, 256), (3, 3, 1, 256, 512)]
-EARLY = 6
+EARLY = 10
 PLAN = [
+    ([[], [], [], []], 'A3'),
+    ([[], [], ['z0'], ['z0']], 'A1'),
     ([[], [], [], []], 'A2'),
-    ([[], [], [], []], 'A1'),
-    ([[], [], [], []], 'A3'),
-    ([[], [], [], []], 'A0'),
-    ([['B0'], ['B0'], ['z0', 'z1', 'z2'], ['z0', 'z1', 'z2']], 'A4'),
-    ([['v0'], ['v0'], ['v0', 'z3'], ['v0', 'z3']], 'A5'),
-    ([['v1', 'x0'], ['v1', 'x0'], ['v1', 'x0', 'z4'], ['v1', 'x0', 'z4']], 'A6'),
+    ([[], [], ['z1'], ['z1']], 'A0'),
+    ([['B2', 'B0'], ['B2', 'B0'], ['B0', 'z2', 'z3'], ['B0', 'z2', 'C0', 'z3']], 'A4'),
+    ([['v0'], ['v0'], ['v0', 'z4', 'z5'], ['v0', 'D0', 'z4', 'z5']], 'A5'),
+    ([['v1', 'x0'], ['v1', 'x0'], ['v1', 'x0', 'D0', 'z6', 'z7'], ['v1', 'x0', 'z6', 'z7']], 'A6'),
     ([['v2'], ['v2'], ['v2'], ['v2']], 'A7'),
-    ([[], [], ['z5'], ['z5']], 'A8'),
+    ([[], [], ['z8', 'z9'], ['z8', 'z9']], 'A8'),
     ([['v3'], ['v3'], ['v3'], ['v3']], 'A9'),
-    ([['x1', 'B2'], ['x1', 'B2'], ['x1', 'B2'], ['x1', 'B2']], 'A16'),
+    ([['x1'], ['x1'], ['x1'], ['x1']], 'A16'),
     ([['B16'], ['B16'], ['B16'], ['B16']], 'A19'),
     ([[], [], [], []], 'A10'),
     ([['B19'], ['B19'], ['B19'], ['B19']], 'A20'),
     ([[], [], [], []], 'A11'),
-    ([['B20', 'B11', 'x2', 'B1', 'B3'], ['B20', 'B11', 'x2', 'B1', 'B3'], ['x2', 'B1', 'B3', 'B0', 'B20'], ['x2', 'B1', 'B3', 'B0', 'B20']], 'A17'),
+    ([['B20', 'B11', 'x2', 'B3', 'B1'], ['B20', 'B11', 'x2', 'B3', 'B1'], ['x2', 'B3', 'B1', 'B2', 'B20'], ['B20', 'x2', 'B3', 'B1', 'B2']], 'A17'),
     ([['B17'], ['B17'], ['B11', 'B17'], ['B11', 'B17']], 'A12'),
     ([[], [], [], []], 'A13'),
-    ([['B12', 'B13'], ['B12', 'B13'], ['B12', 'B13'], ['B12', 'B13']], 'A21'),
+    ([[], [], ['B12', 'B13'], ['B12', 'B13']], 'A21'),
     ([['B21'], ['B21'], ['B21'], ['B21']], 'A14'),
     ([[], [], [], []], 'A15'),
-    ([['x3', 'B10', 'B6', 'B7', 'D0', 'B5', 'B8', 'B9', 'B4', 'B14', 'B15'], ['C0', 'D0', 'C2', 'x3', 'B10', 'B6', 'B7', 'B5', 'B8', 'B9', 'B4', 'B14', 'B15'], ['B14', 'x3', 'B10', 'B6', 'B7', 'B5', 'B8', 'B9', 'B4', 'B15'], ['B14', 'x3', 'B10', 'B6', 'B7', 'B5', 'B8', 'B9', 'B4', 'B15']], 'A18'),
-    ([['B18', 'D2'], ['D2', 'B18', 'C16', 'C19', 'C20', 'D16', 'C11'], ['B18', 'D2'], ['B18', 'C2', 'D2', 'C16']], 'A22'),
-    ([[], [], [], ['C19']], 'A23'),
-    ([['B22', 'B23', 'D16'], ['C1'], ['B22', 'B23', 'D16'], ['C1', 'B22', 'B23', 'C3', 'D16', 'C0']], 'E16'),
-    ([['D19'], ['D19', 'B22', 'B23', 'C3', 'D20'], ['D19', 'D1'], ['D19', 'D1', 'C20']], 'E19'),
-    ([['D20'], [], ['D3', 'D0', 'D20'], ['D3', 'C11', 'D0', 'C17', 'D20', 'C12', 'C13']], 'E20'),
-    ([['D11', 'D1', 'D3'], ['D11', 'C17', 'C12', 'D1', 'C13', 'D3', 'C21'], [], []], 'E3'),
-    ([[], [], ['D11'], ['D11', 'C21', 'C14', 'D17']], 'E11'),
-    ([['D17', 'D12'], ['D17', 'D12', 'C10', 'C6', 'D13'], ['D17', 'D12'], ['D12']], 'E17'),
-    ([['D13'], ['C7'], ['D13'], ['D13', 'C10', 'C6']], 'E13'),
-    ([['D21'], ['D21', 'C5'], ['D21', 'D14'], ['D21', 'C7', 'D14']], 'E21'),
-    ([['D10', 'D6'], ['D10', 'C8', 'C9', 'D6'], ['D10', 'D6'], ['C5', 'C8', 'D10', 'C9', 'D6']], 'E10'),
-    ([['D7'], ['D7', 'C4'], ['D7'], ['D7', 'C4']], 'E7'),
-    ([['D5', 'D8'], ['D5', 'C14', 'C15', 'D8'], ['D5', 'D8'], ['D5', 'C15', 'D8']], 'E5'),
-    ([['D9'], ['D9', 'C18'], ['D9'], ['D9', 'C18', 'C22']], 'E9'),
-    ([['D4', 'D14'], ['D4', 'C22', 'C23', 'D14'], ['D4', 'D15'], ['D4', 'C23', 'D15']], 'E4'),
-    ([['D15'], ['D15'], [], []], 'E15'),
+    ([['x3', 'B6', 'B7', 'B12', 'B13', 'B10', 'B5', 'B8', 'B9', 'B4', 'B14', 'B15'], ['C2', 'C0', 'x3', 'B6', 'B7', 'B12', 'B13', 'B10', 'B5', 'B8', 'B9', 'B4', 'B14', 'B15'], ['x3', 'B6', 'B7', 'B10', 'B5', 'B8', 'B9', 'B4', 'B14', 'B15'], ['x3', 'B6', 'B7', 'B10', 'B5', 'B8', 'B9', 'B4', 'B14', 'B15']], 'A18'),
+    ([['B18', 'D2', 'D0'], ['D2', 'D0', 'B18', 'C16', 'C19', 'C20', 'D16', 'C11'], ['B18'], ['B18', 'C16', 'C19']], 'A22'),
+    ([[], [], [], ['C3']], 'A23'),
+    ([['B22', 'B23', 'D16'], [], ['B22', 'B23', 'D16'], ['B22', 'C1', 'D16', 'B23', 'C2']], 'E16'),
+    ([['D19'], ['D19', 'C3', 'B22', 'B23', 'C1', 'D20'], ['D19'], ['D19', 'C20', 'D3']], 'E19'),
+    ([['D20'], [], ['D3', 'D1', 'D2', 'D20'], ['D1', 'C11', 'D2', 'C17', 'D20', 'C12', 'C13', 'D11']], 'E20'),
+    ([['D11', 'D3', 'D1'], ['D11', 'C17', 'D3', 'C21', 'C6', 'D1', 'C7'], [], []], 'E3'),
+    ([[], [], ['D11'], ['C21']], 'E11'),
+    ([['D17'], ['D17', 'C12', 'C13'], ['D17', 'D12'], ['D17', 'C6', 'C7', 'D12']], 'E17'),
+    ([['D21', 'D6'], ['D21', 'D6', 'C10', 'D7'], ['D13', 'D21', 'D6'], ['D13', 'C10', 'D21', 'C5', 'D6']], 'E21'),
+    ([['D7', 'D12', 'D13'], ['D12', 'C5', 'D13', 'C8', 'C9'], [], []], 'E13'),
+    ([[], [], ['D7'], ['D7', 'C8', 'C9']], 'E7'),
+    ([['D10'], ['D10', 'C4'], ['D10'], ['D10', 'C4']], 'E10'),
+    ([['D5', 'D8'], ['D5', 'C14', 'C15', 'D8'], ['D5', 'D8'], ['D5', 'C14', 'C15', 'D8']], 'E5'),
+    ([['D9'], ['D9', 'C18'], ['D9'], ['D9', 'C18']], 'E9'),
+    ([['D4', 'D14'], ['D4', 'C22', 'C23', 'D14'], ['D4', 'D14'], ['D4', 'C22', 'C23', 'D14']], 'E4'),
+    ([['D15'], ['D15'], ['D15'], ['D15']], 'E15'),
     ([['D18', 'D22'], ['D18', 'D22'], ['D18', 'D22'], ['D18', 'D22']], 'E18'),
     ([['D23'], ['D23'], ['D23'], ['D23']], 'E23'),
 ]
 
-PIECES = [(0, 0, 256), (0, 256, 256), (0, 512, 512 + PAD), (1, 0, 1024), (2, 0, 1024), (3, 0, 1024)]
+PIECES = [(0, 0, 128), (0, 128, 128), (0, 256, 256), (0, 512, 512 + PAD), (1, 0, 512), (1, 512, 512), (2, 0, 512), (2, 512, 512), (3, 0, 512), (3, 512, 512)]
 
 
 def split(value):

time: 183 us -> 188 us (1.027)
  Pallas kernels: 179 us -> 182 us
    pallas_call x1, Pallas kernels: 178 us -> 181 us  [on_device(): pl.pallas_call(lambda *refs: kernel(sizes, *refs), name='ri_mp2', out_sha...]
where the time goes in v4:
time: 188 us; the launch traced here: 186 us
  Pallas kernels  182 us (97%)
  local copies, waits for them, and re-layouts  2.92 us (2%)
    pallas_call x1, Pallas kernels, on_device(): pl.pallas_call(lambda *refs: kernel(sizes, *refs), name='ri_mp2', out_sha...  181 us

profile of v4, /device:TPU:2, one launch (start us, length us, event | category | flops | bytes accessed | tf_op | source)
XLA Modules:
  0.0 185.9 jit_solution(18194155481218473033)
XLA Ops:
  0.7 0.0 copy-start
  0.7 1.6 copy-done
  2.2 0.0 copy-start.1
  2.2 0.7 copy-done.1
  2.9 0.0 copy-start.2
  2.9 0.7 copy-done.2
  3.6 180.7 %ri_mp2.1.source = f32[4096,128]{1,0:T(8,128)S(1)} custom-call(f32[4096,128]{1,0:T(8,128)S(1)} %bitcast.3, f32[4,128]{1,0:T(4,128)S(1)} %bitcast.4, f32[1]{0:T(128)S(6)} %copy.6.refs_2_, s32[1,4]{1,0:T(1,128)S(1)} %copy-done.2), custom_call_target="tpu_custom_call" | custom-call | tf_op jit(solution)/shard_map/ri_mp2/pallas_call | solution.py:425
  184.3 1.4 write_out.1
Async XLA Ops:
  0.7 1.6 copy-start
  2.2 0.7 copy-start.1
  2.9 0.7 copy-start.2
